TPU v7x, 32 devices: a whole 2x2x4 slice. The times are simulated.
32 devices in a mesh: row: 4 (over y, x), col: 8 (over z, core).
Axes of the slice: x: 2, y: 2, z: 4, core: 2. Of those that a mesh axis runs over, the one named last changes fastest.
Arguments:
- tokens: bfloat16 [1024, 53248], P(('row', 'col')), may hold values from -6 to 6
- eigvecs: float32 [53248, 2048], P('row', 'col'), may hold values from -0.02734375 to 0.02734375
- eigvals: float32 [2048], P('col'), may hold values from 0.25 to 4
- v_first: float32 [53248, 256], P(('row', 'col')), may hold values from -0.109375 to 0.109375
- v_second: float32 [53248, 256], P(('row', 'col')), may hold values from -0.109375 to 0.109375
- t_first: float32 [256, 256], replicated, may hold values from -0.375 to 0.375
- t_second: float32 [256, 256], replicated, may hold values from -0.375 to 0.375
Outputs:
- whitened: float32 [1024, 2048], P('row', 'col')
All inputs are finite; a program needn't handle non-finite values.
Results may differ from a plain program's by a relative error of at most 0.0029.
Values may be sent and summed in bfloat16 or wider, within the bound.
No kernel may reach another device: no remote copies, remote signals or barrier semaphores. Data moves between devices by JAX's collectives and lax.ppermute only.
A program may use at most 128 MiB of HBM per device.

v0:
```python
import jax
import jax.numpy as jnp
from jax import lax
from jax.sharding import PartitionSpec as P

HIGHEST = lax.Precision.HIGHEST
CHUNKS = 2


def dot32(a, b):
    return jnp.dot(a, b, precision=HIGHEST, preferred_element_type=jnp.float32)


def dot16(a, b):
    return jnp.dot(a, b, preferred_element_type=jnp.float32)


def split(v):
    high = lax.reduce_precision(v, 8, 7)
    return (high.astype(jnp.bfloat16), (v - high).astype(jnp.bfloat16))


def make(rows, cols):
    swap = [(i, i ^ 1) for i in range(cols)]
    groups = [[i for i in range(cols) if i % 2 == core] for core in range(2)]
    half = cols // 2

    def row_sum(x):
        return jnp.sum(lax.all_to_all(x, "row", split_axis=0, concat_axis=0, tiled=True), axis=0)

    def core_sum(parts, core):
        even = jnp.stack(parts[0::2])
        odd = jnp.stack(parts[1::2])
        mine = jnp.where(core == 0, even, odd)
        other = jnp.where(core == 0, odd, even)
        return mine + lax.ppermute(other, "col", swap)

    def z_sum(x):
        got = lax.all_to_all(
            x, "col", split_axis=0, concat_axis=0, tiled=True, axis_index_groups=groups
        )
        return jnp.sum(got, axis=0)

    def per_device(tokens, eigvecs, eigvals, v_first, v_second, t_first, t_second):
        nb = v_first.shape[1]
        core = lax.axis_index("col") % 2
        slab = lax.all_to_all(tokens, ("row", "col"), split_axis=1, concat_axis=0, tiled=True)
        tok = slab.shape[0]
        depth, width = (v_first.shape[0], eigvecs.shape[1])
        high, low = split(jnp.concatenate([v_first, v_second], axis=1))
        along = dot16(slab, high) + dot16(slab, low)
        gram = dot32(v_first.T, v_second)
        packed = jnp.concatenate(
            [
                along.reshape(rows, tok // rows, 2 * nb),
                jnp.broadcast_to(gram.reshape(1, nb // 2, 2 * nb), (rows, nb // 2, 2 * nb)),
            ],
            axis=1,
        )
        packed = packed.reshape(rows * packed.shape[1], 2 * nb)
        packed = lax.psum(lax.psum_scatter(packed, "row", scatter_dimension=0, tiled=True), "col")
        along = packed[: tok // rows]
        gram = packed[tok // rows :].reshape(nb, nb)
        outs = []
        step = width // CHUNKS
        for j in range(CHUNKS):
            piece = (
                eigvecs[:, j * step : (j + 1) * step]
                .astype(jnp.bfloat16)
                .reshape(cols, depth, step)
            )
            piece = lax.all_to_all(piece, "col", split_axis=0, concat_axis=0, tiled=True)
            parts = []
            for s in range(cols):
                w = piece[s]
                p = dot16(slab, w)
                i = dot16(high.T, w) + dot16(low.T, w)
                parts.append(
                    jnp.concatenate(
                        [p.reshape(rows, tok // rows, step), i.reshape(rows, 2 * nb // rows, step)],
                        axis=1,
                    )
                )
            summed = core_sum(parts, core)
            summed = row_sum(jnp.swapaxes(summed, 0, 1))
            summed = z_sum(summed)
            base = summed[: tok // rows]
            inner = summed[tok // rows :]
            inner = lax.all_to_all(
                jnp.broadcast_to(inner[None], (rows, *inner.shape)),
                "row",
                split_axis=0,
                concat_axis=0,
                tiled=True,
            )
            inner = inner.reshape(2 * nb, step)
            m_second = dot32(t_second, inner[nb:])
            m_first = dot32(t_first, inner[:nb] - dot32(gram, m_second))
            scale = lax.rsqrt(eigvals[j * step : (j + 1) * step])
            outs.append(
                (base - dot32(along[:, nb:], m_second) - dot32(along[:, :nb], m_first))
                * scale[None, :]
            )
        return jnp.concatenate(outs, axis=1)

    return per_device


def solution(mesh):
    in_specs = (
        P(("row", "col"), None),
        P("row", "col"),
        P("col"),
        P(("row", "col"), None),
        P(("row", "col"), None),
        P(),
        P(),
    )
    out_specs = P("row", "col")
    body = make(mesh.shape["row"], mesh.shape["col"])
    return jax.shard_map(body, mesh=mesh, in_specs=in_specs, out_specs=out_specs, check_vma=False)
```

profile of v0, /device:TPU:0, one launch (start us, length us, event | category | flops | bytes accessed | tf_op | source)
XLA Modules:
  0.0 556.7 jit_solution(4502269078186748890)
XLA Ops:
  6.5 5.5 convert.4
  14.0 83.4 %all_to_all.59 = bf16[8,1664,128]{2,1,0:T(8,128)(2,1)} all-to-all(bf16[8,1664,128]{2,1,0:T(8,128)(2,1)S(1)} %bitcast.272), channel_id=1, replica_groups=mesh['row'=4,'col'=8] {'col'}, dimensions={0} | all-to-all | bytes 6815744 | tf_op jit(solution)/shard_map/all_to_all | solution.py:72
  97.3 4.5 all-to-all-start.5
  101.8 4.2 copy.39
  116.9 62.0 %all-to-all-done.5 = bf16[8,1664,128]{2,1,0:T(8,128)(2,1)} async-done(((bf16[8,1664,128]{2,1,0:T(8,128)(2,1)}), bf16[8,1664,128]{2,1,0:T(8,128)(2,1)}, u32[]{:S(2)}, u32[]{:S(2)}) %all-to-all-start.5) | async-done | bytes 3407904 | tf_op jit(solution)/shard_map/all_to_all | solution.py:72
  179.0 3.8 all-to-all-start
  226.9 33.8 %all-to-all-done = bf16[32,32,1664]{2,0,1:T(8,128)(2,1)} async-done(((bf16[32,32,1664]{2,0,1:T(8,128)(2,1)}), bf16[32,32,1664]{2,0,1:T(8,128)(2,1)}, u32[]{:S(2)}, u32[]{:S(2)}) %all-to-all-start) | async-done | bytes 3407904 | tf_op jit(solution)/shard_map/all_to_all | solution.py:47
  260.7 3.2 fusion.75
  273.5 3.6 fusion.55
  280.3 3.6 fusion.45
  299.0 3.1 fusion.30
  303.3 3.6 fusion.15
  307.0 3.1 fusion.20
  310.3 3.6 fusion.10
  313.9 3.1 fusion.5
  320.9 3.7 fusion.141
  328.2 6.1 %fusion.140 = f32[512,1024]{1,0:T(8,128)} fusion(bf16[1664,512]{1,0:T(8,128)(2,1)} %copy-done.1, bf16[1024,1664]{1,0:T(8,128)(2,1)} %bitcast.37), kind=kOutput, calls=%fused_computation.194 | convolution fusion | flops 1744830464 | bytes 7208960 | tf_op jit(solution)/shard_map/dot_general | solution.py:15
  338.6 4.7 all-to-all-start.2
  343.3 6.1 %add_bitcast_fusion.2 = f32[1024,512]{0,1:T(8,128)} fusion(f32[512,1024]{1,0:T(8,128)} %fusion.140, bf16[1664,512]{1,0:T(8,128)(2,1)S(1)} %get-tuple-element.7, bf16[1024,1664]{1,0:T(8,128)(2,1)} %bitcast.37), kind=kOutput, calls=%fused_computation.11 | convolution fusion | flops 1745354752 | bytes 9306112 | tf_op jit(solution)/shard_map/dot_general | solution.py:15
  349.4 3.2 reshape.135
  364.9 30.8 %all-to-all-done.2 = f32[4,4,384,128]{3,2,1,0:T(8,128)} async-done(((f32[4,4,384,128]{3,2,1,0:T(8,128)}), f32[4,4,384,128]{3,2,1,0:T(8,128)}, u32[]{:S(2)}, u32[]{:S(2)}) %all-to-all-start.2) | async-done | bytes 3145760 | tf_op jit(solution)/shard_map/all_to_all | solution.py:29
  395.6 3.7 all-to-all-start.6
  399.4 3.2 reduce_sum.36
  402.6 40.4 %all-to-all-done.6 = f32[4,4,384,128]{3,2,1,0:T(8,128)S(1)} async-done(((f32[4,4,384,128]{3,2,1,0:T(8,128)}), f32[4,4,384,128]{3,2,1,0:T(8,128)S(1)}, u32[]{:S(2)}, u32[]{:S(2)}) %all-to-all-start.6) | async-done | bytes 3145760 | tf_op jit(solution)/shard_map/all_to_all | solution.py:29
  443.0 4.2 all-to-all-start.3
  448.3 18.5 %all-to-all-done.3 = f32[4,384,128]{2,1,0:T(8,128)} async-done(((f32[4,384,128]{2,1,0:T(8,128)}), f32[4,384,128]{2,1,0:T(8,128)}, u32[]{:S(2)}, u32[]{:S(2)}) %all-to-all-start.3) | async-done | bytes 786464 | tf_op jit(solution)/shard_map/all_to_all | solution.py:39
  466.9 3.5 all-to-all-start.7
  472.3 21.1 %all-to-all-done.7 = f32[4,384,128]{2,1,0:T(8,128)S(1)} async-done(((f32[4,384,128]{2,1,0:T(8,128)}), f32[4,384,128]{2,1,0:T(8,128)S(1)}, u32[]{:S(2)}, u32[]{:S(2)}) %all-to-all-start.7) | async-done | bytes 786464 | tf_op jit(solution)/shard_map/all_to_all | solution.py:39
  494.2 3.4 all-to-all-start.4
  497.7 36.4 %all-reduce.2.cloned.1.call-done = f32[384,512]{1,0:T(8,128)} async-done(((f32[384,512]{1,0:T(8,128)}), f32[384,512]{1,0:T(8,128)}) %all-reduce.2.cloned.1.call-update) | async-done | bytes 786448 | tf_op jit(solution)/shard_map/psum | solution.py:61
  536.1 3.6 all-to-all-start.8
  540.2 4.9 all-to-all-done.8
  (213 shorter events, 119.9 us)
Async XLA Ops:
  6.5 533.3 %copy-start = (f32[256,256]{1,0:T(8,128)S(1)}, f32[256,256]{1,0:T(8,128)}, u32[]{:S(2)}) copy-start(f32[256,256]{1,0:T(8,128)} %param.13) | copy-start | bytes 786436
  97.3 81.6 %all-to-all-start.5 = ((bf16[8,1664,128]{2,1,0:T(8,128)(2,1)}), bf16[8,1664,128]{2,1,0:T(8,128)(2,1)}, u32[]{:S(2)}, u32[]{:S(2)}) async-start(bf16[8,1664,128]{2,1,0:T(8,128)(2,1)} %bitcast.271), calls=%async_computation.6 | async-start | bytes 6815744 | tf_op jit(solution)/shard_map/all_to_all | solution.py:72
  108.2 8.0 %copy-start.1 = (bf16[1664,512]{1,0:T(8,128)(2,1)}, bf16[1664,512]{1,0:T(8,128)(2,1)S(1)}, u32[]{:S(2)}) copy-start(bf16[1664,512]{1,0:T(8,128)(2,1)S(1)} %get-tuple-element.8) | copy-start | bytes 5111812
  179.0 81.7 %all-to-all-start = ((bf16[32,32,1664]{2,0,1:T(8,128)(2,1)}), bf16[32,32,1664]{2,0,1:T(8,128)(2,1)}, u32[]{:S(2)}, u32[]{:S(2)}) async-start(bf16[32,32,1664]{2,0,1:T(8,128)(2,1)} %bitcast.270), calls=%async_computation | async-start | bytes 6815744 | tf_op jit(solution)/shard_map/all_to_all | solution.py:47
  273.4 13.7 %copy-start.10 = (f32[1,4,384,128]{3,2,1,0:T(8,128)}, f32[1,4,384,128]{3,2,1,0:T(8,128)S(1)}, u32[]{:S(2)}) copy-start(f32[1,4,384,128]{3,2,1,0:T(8,128)S(1)} %get-tuple-element.25) | copy-start | bytes 2359300
  273.4 13.7 %copy-start.12 = (f32[1,4,384,128]{3,2,1,0:T(8,128)}, f32[1,4,384,128]{3,2,1,0:T(8,128)S(1)}, u32[]{:S(2)}) copy-start(f32[1,4,384,128]{3,2,1,0:T(8,128)S(1)} %get-tuple-element.26) | copy-start | bytes 2359300
  280.3 6.9 %copy-start.18 = (f32[1,4,384,128]{3,2,1,0:T(8,128)}, f32[1,4,384,128]{3,2,1,0:T(8,128)S(1)}, u32[]{:S(2)}) copy-start(f32[1,4,384,128]{3,2,1,0:T(8,128)S(1)} %get-tuple-element.27) | copy-start | bytes 2359300
  280.3 6.9 %copy-start.20 = (f32[1,4,384,128]{3,2,1,0:T(8,128)}, f32[1,4,384,128]{3,2,1,0:T(8,128)S(1)}, u32[]{:S(2)}) copy-start(f32[1,4,384,128]{3,2,1,0:T(8,128)S(1)} %get-tuple-element.28) | copy-start | bytes 2359300
  289.6 44.6 %collective-permute-start = (f32[4,4,384,128]{3,2,1,0:T(8,128)}, f32[4,4,384,128]{3,2,1,0:T(8,128)}, u32[]{:S(2)}, u32[]{:S(2)}) collective-permute-start(f32[4,4,384,128]{3,2,1,0:T(8,128)} %fusion.2), channel_id=1, source_target_pairs={{0,1},{1,0},{2,3},{3,2},{4,5},{5,4},{6,7},{7,6},{8,9},{9,8},{10,11... | collective-permute-start | bytes 9437192 | tf_op jit(solution)/shard_map/ppermute | solution.py:36
  302.3 14.9 %copy-start.6 = (f32[1,4,384,128]{3,2,1,0:T(8,128)}, f32[1,4,384,128]{3,2,1,0:T(8,128)S(1)}, u32[]{:S(2)}) copy-start(f32[1,4,384,128]{3,2,1,0:T(8,128)S(1)} %get-tuple-element.15) | copy-start | bytes 2359300
  302.3 14.9 %copy-start.8 = (f32[1,4,384,128]{3,2,1,0:T(8,128)}, f32[1,4,384,128]{3,2,1,0:T(8,128)S(1)}, u32[]{:S(2)}) copy-start(f32[1,4,384,128]{3,2,1,0:T(8,128)S(1)} %get-tuple-element.16) | copy-start | bytes 2359300
  303.3 14.0 %copy-start.14 = (f32[1,4,384,128]{3,2,1,0:T(8,128)}, f32[1,4,384,128]{3,2,1,0:T(8,128)S(1)}, u32[]{:S(2)}) copy-start(f32[1,4,384,128]{3,2,1,0:T(8,128)S(1)} %get-tuple-element.17) | copy-start | bytes 2359300
  303.3 14.0 %copy-start.16 = (f32[1,4,384,128]{3,2,1,0:T(8,128)}, f32[1,4,384,128]{3,2,1,0:T(8,128)S(1)}, u32[]{:S(2)}) copy-start(f32[1,4,384,128]{3,2,1,0:T(8,128)S(1)} %get-tuple-element.18) | copy-start | bytes 2359300
  310.2 7.0 %copy-start.22 = (f32[1,4,384,128]{3,2,1,0:T(8,128)}, f32[1,4,384,128]{3,2,1,0:T(8,128)S(1)}, u32[]{:S(2)}) copy-start(f32[1,4,384,128]{3,2,1,0:T(8,128)S(1)} %get-tuple-element.19) | copy-start | bytes 2359300
  310.3 7.0 %copy-start.23 = (f32[1,4,384,128]{3,2,1,0:T(8,128)}, f32[1,4,384,128]{3,2,1,0:T(8,128)S(1)}, u32[]{:S(2)}) copy-start(f32[1,4,384,128]{3,2,1,0:T(8,128)S(1)} %get-tuple-element.20) | copy-start | bytes 2359300
  319.6 38.6 %collective-permute-start.1 = (f32[4,4,384,128]{3,2,1,0:T(8,128)}, f32[4,4,384,128]{3,2,1,0:T(8,128)}, u32[]{:S(2)}, u32[]{:S(2)}) collective-permute-start(f32[4,4,384,128]{3,2,1,0:T(8,128)} %fusion.1), channel_id=1, source_target_pairs={{0,1},{1,0},{2,3},{3,2},{4,5},{5,4},{6,7},{7,6},{8,9},{9,8},{10,11... | collective-permute-start | bytes 9437192 | tf_op jit(solution)/shard_map/ppermute | solution.py:36
  328.1 6.1 %copy-start.13 = (f32[1,4,384,128]{3,2,1,0:T(8,128)S(1)}, f32[1,4,384,128]{3,2,1,0:T(8,128)}, u32[]{:S(2)}) copy-start(f32[1,4,384,128]{3,2,1,0:T(8,128)} %copy-done.12) | copy-start | bytes 2359300
  328.2 6.1 %copy-start.19 = (f32[1,4,384,128]{3,2,1,0:T(8,128)S(1)}, f32[1,4,384,128]{3,2,1,0:T(8,128)}, u32[]{:S(2)}) copy-start(f32[1,4,384,128]{3,2,1,0:T(8,128)} %copy-done.18) | copy-start | bytes 2359300
  328.2 6.1 %copy-start.21 = (f32[1,4,384,128]{3,2,1,0:T(8,128)S(1)}, f32[1,4,384,128]{3,2,1,0:T(8,128)}, u32[]{:S(2)}) copy-start(f32[1,4,384,128]{3,2,1,0:T(8,128)} %copy-done.20) | copy-start | bytes 2359300
  328.2 6.1 %copy-start.25 = (f32[1,4,384,128]{3,2,1,0:T(8,128)S(1)}, f32[1,4,384,128]{3,2,1,0:T(8,128)}, u32[]{:S(2)}) copy-start(f32[1,4,384,128]{3,2,1,0:T(8,128)} %copy-done.24) | copy-start | bytes 2359300
  328.2 6.1 %copy-start.27 = (f32[1,4,384,128]{3,2,1,0:T(8,128)S(1)}, f32[1,4,384,128]{3,2,1,0:T(8,128)}, u32[]{:S(2)}) copy-start(f32[1,4,384,128]{3,2,1,0:T(8,128)} %copy-done.26) | copy-start | bytes 2359300
  338.6 57.1 %all-to-all-start.2 = ((f32[4,4,384,128]{3,2,1,0:T(8,128)}), f32[4,4,384,128]{3,2,1,0:T(8,128)}, u32[]{:S(2)}, u32[]{:S(2)}) async-start(f32[4,4,384,128]{3,2,1,0:T(8,128)} %copy.28), calls=%async_computation.2 | async-start | bytes 6291456 | tf_op jit(solution)/shard_map/all_to_all | solution.py:29
  343.3 127.2 %reduce-scatter.2.cloned.1.call-start = ((), (), s32[]{:S(2)}) async-start(), calls=%async_computation.10 | async-start | bytes 3932160 | tf_op jit(solution)/shard_map/reduce_scatter | solution.py:61
  395.6 47.3 %all-to-all-start.6 = ((f32[4,4,384,128]{3,2,1,0:T(8,128)}), f32[4,4,384,128]{3,2,1,0:T(8,128)S(1)}, u32[]{:S(2)}, u32[]{:S(2)}) async-start(f32[4,4,384,128]{3,2,1,0:T(8,128)} %copy.32), calls=%async_computation.7 | async-start | bytes 6291456 | tf_op jit(solution)/shard_map/all_to_all | solution.py:29
  443.0 23.9 %all-to-all-start.3 = ((f32[4,384,128]{2,1,0:T(8,128)}), f32[4,384,128]{2,1,0:T(8,128)}, u32[]{:S(2)}, u32[]{:S(2)}) async-start(f32[4,384,128]{2,1,0:T(8,128)} %reduce_sum.36), calls=%async_computation.3 | async-start | bytes 1572864 | tf_op jit(solution)/shard_map/all_to_all | solution.py:39
  448.3 49.3 %copy-start.55 = (f32[256]{0:T(256)S(1)}, f32[256]{0:T(256)}, u32[]{:S(2)}) copy-start(f32[256]{0:T(256)} %param.9) | copy-start | bytes 3076
  466.9 26.6 %all-to-all-start.7 = ((f32[4,384,128]{2,1,0:T(8,128)}), f32[4,384,128]{2,1,0:T(8,128)S(1)}, u32[]{:S(2)}, u32[]{:S(2)}) async-start(f32[4,384,128]{2,1,0:T(8,128)} %reduce_sum.38), calls=%async_computation.8 | async-start | bytes 1572864 | tf_op jit(solution)/shard_map/all_to_all | solution.py:39
  470.4 63.8 %all-reduce.2.cloned.1.call-start = ((), (), s32[]{:S(2)}) async-start(), calls=%async_computation.11 | async-start | bytes 1572864 | tf_op jit(solution)/shard_map/psum | solution.py:61
  494.2 41.2 %all-to-all-start.4 = ((f32[4,128,128]{2,1,0:T(8,128)}), f32[4,128,128]{2,1,0:T(8,128)S(1)}, u32[]{:S(2)}, u32[]{:S(2)}) async-start(f32[4,128,128]{2,1,0:T(8,128)} %broadcast_in_dim.10), calls=%async_computation.5 | async-start | bytes 524288 | tf_op jit(solution)/shard_map/all_to_all | solution.py:89
  497.6 48.3 %copy-start.54 = (f32[256,256]{1,0:T(8,128)S(1)}, f32[256,256]{1,0:T(8,128)}, u32[]{:S(2)}) copy-start(f32[256,256]{1,0:T(8,128)} %param.12) | copy-start | bytes 786436
  535.1 12.0 %copy-start.36 = (f32[384,512]{1,0:T(8,128)S(1)}, f32[384,512]{1,0:T(8,128)}, u32[]{:S(2)}) copy-start(f32[384,512]{1,0:T(8,128)} %all-reduce.2.cloned.1.call-done) | copy-start | bytes 2359300
  536.1 9.0 %all-to-all-start.8 = ((f32[4,128,128]{2,1,0:T(8,128)}), f32[4,128,128]{2,1,0:T(8,128)S(1)}, u32[]{:S(2)}, u32[]{:S(2)}) async-start(f32[4,128,128]{2,1,0:T(8,128)} %broadcast_in_dim.11), calls=%async_computation.9 | async-start | bytes 524288 | tf_op jit(solution)/shard_map/all_to_all | solution.py:89
  (36 other events, 100.8 us)
Sparse Core Ops, SparseCore 0:
  358.3 78.5 reduce-scatter.1
  473.5 60.5 all-reduce.1
where the time goes:
time: 564 us; the launch traced here: 557 us
  waiting for transfers between devices  249 us (44%)
  matrix products  122 us (22%)
  blocking collectives  83.4 us (15%)
  starting transfers between devices  32.1 us (6%)
  local copies, waits for them, and re-layouts  31 us (5%)
  other arithmetic  24.5 us (4%)
  between operations  14.8 us (3%)
    dot_general x50, matrix products, dot16(): return jnp.dot(a, b, preferred_element_type=jnp.float32)  114 us
    all_to_all x1, blocking collectives, per_device(): lax.all_to_all(piece, 'col', split_axis=0, concat_axis=0, tiled=True)  83.4 us
    all_to_all x2, waiting for transfers between devices, row_sum(): lax.all_to_all(x, 'row', split_axis=0, concat_axis=0, tiled=True)  71.1 us
    all_to_all x1, waiting for transfers between devices, per_device(): lax.all_to_all(piece, 'col', split_axis=0, concat_axis=0, tiled=True)  62 us
    all_to_all x2, waiting for transfers between devices, z_sum(): lax.all_to_all(x, 'col', split_axis=0, concat_axis=0, tiled=True, axis_in...  39.7 us
    psum x1, waiting for transfers between devices, per_device(): lax.psum(lax.psum_scatter(packed, 'row', scatter_dimension=0, tiled=True)...  36.4 us
    all_to_all x1, waiting for transfers between devices, per_device(): lax.all_to_all(tokens, ('row', 'col'), split_axis=1, concat_axis=0, tiled...  33.8 us
  transfers between devices with their start and end apart: 12, of which 8 were waited for; matrix products, arithmetic and copies ran while one was open for 23% of the time, Pallas kernels for 0%

commit v1 on v0

--- a/solution.py
+++ b/solution.py
@@ -58,7 +58,10 @@
             axis=1,
         )
         packed = packed.reshape(rows * packed.shape[1], 2 * nb)
-        packed = lax.psum(lax.psum_scatter(packed, "row", scatter_dimension=0, tiled=True), "col")
+        packed = jnp.sum(
+            lax.all_gather(lax.psum_scatter(packed, "row", scatter_dimension=0, tiled=True), "col"),
+            axis=0,
+        )
         along = packed[: tok // rows]
         gram = packed[tok // rows :].reshape(nb, nb)
         outs = []

time: 564 us -> 529 us (0.938)
  waiting for transfers between devices: 249 us -> 209 us
    psum x1 -> x0, waiting for transfers between devices: 36.4 us -> none  [per_device(): lax.psum(lax.psum_scatter(packed, 'row', scatter_dimension=0, tiled=True)...]
    unnamed x115 -> x97, local copies, waits for them, and re-layouts: 7.72 us -> 11.5 us
  transfers between devices with their start and end apart: 12 -> 12, of which waited for: 8 -> 8; matrix products, arithmetic and copies ran while one was open for 23% -> 27% of each run, Pallas kernels for 0% -> 0%
where the time goes in v1:
time: 529 us; the launch traced here: 521 us
  waiting for transfers between devices  209 us (40%)
  matrix products  127 us (24%)
  blocking collectives  83.4 us (16%)
  starting transfers between devices  31.6 us (6%)
  local copies, waits for them, and re-layouts  28.3 us (5%)
  other arithmetic  27 us (5%)
  between operations  14.8 us (3%)
    dot_general x50, matrix products, dot16(): return jnp.dot(a, b, preferred_element_type=jnp.float32)  119 us
    all_to_all x1, blocking collectives, per_device(): lax.all_to_all(piece, 'col', split_axis=0, concat_axis=0, tiled=True)  83.4 us
    all_to_all x2, waiting for transfers between devices, row_sum(): lax.all_to_all(x, 'row', split_axis=0, concat_axis=0, tiled=True)  66.3 us
    all_to_all x1, waiting for transfers between devices, per_device(): lax.all_to_all(piece, 'col', split_axis=0, concat_axis=0, tiled=True)  59 us
    all_to_all x1, waiting for transfers between devices, per_device(): lax.all_to_all(tokens, ('row', 'col'), split_axis=1, concat_axis=0, tiled...  36.8 us
    all_to_all x2, waiting for transfers between devices, z_sum(): lax.all_to_all(x, 'col', split_axis=0, concat_axis=0, tiled=True, axis_in...  36.1 us
    unnamed x97, local copies, waits for them, and re-layouts  11.5 us
  transfers between devices with their start and end apart: 12, of which 8 were waited for; matrix products, arithmetic and copies ran while one was open for 27% of the time, Pallas kernels for 0%

profile of v1, /device:TPU:0, one launch (start us, length us, event | category | flops | bytes accessed | tf_op | source)
XLA Modules:
  0.0 520.6 jit_solution(5650583678820597720)
XLA Ops:
  6.5 5.5 %convert.4 = bf16[13312,256]{1,0:T(8,128)(2,1)S(1)} convert(f32[13312,256]{1,0:T(8,128)} %param.8) | non-fusion elementwise | flops 3407872 | bytes 20447232 | tf_op jit(solution)/shard_map/convert.1
  14.1 83.4 %all_to_all.59 = bf16[8,1664,128]{2,1,0:T(8,128)(2,1)} all-to-all(bf16[8,1664,128]{2,1,0:T(8,128)(2,1)S(1)} %bitcast.280), channel_id=1, replica_groups=mesh['row'=4,'col'=8] {'col'}, dimensions={0} | all-to-all | bytes 6815744 | tf_op jit(solution)/shard_map/all_to_all | solution.py:75
  97.5 4.6 all-to-all-start.5
  102.1 4.3 fusion.141
  107.3 3.9 copy.42
  120.2 59.0 %all-to-all-done.5 = bf16[8,1664,128]{2,1,0:T(8,128)(2,1)} async-done(((bf16[8,1664,128]{2,1,0:T(8,128)(2,1)}), bf16[8,1664,128]{2,1,0:T(8,128)(2,1)}, u32[]{:S(2)}, u32[]{:S(2)}) %all-to-all-start.5) | async-done | bytes 3407904 | tf_op jit(solution)/shard_map/all_to_all | solution.py:75
  179.2 3.6 all-to-all-start
  224.2 36.8 %all-to-all-done = bf16[32,32,1664]{2,0,1:T(8,128)(2,1)} async-done(((bf16[32,32,1664]{2,0,1:T(8,128)(2,1)}), bf16[32,32,1664]{2,0,1:T(8,128)(2,1)}, u32[]{:S(2)}, u32[]{:S(2)}) %all-to-all-start) | async-done | bytes 3407904 | tf_op jit(solution)/shard_map/all_to_all | solution.py:47
  260.9 4.6 fusion.140
  265.5 5.4 %add_bitcast_fusion.2 = f32[1024,512]{0,1:T(8,128)} fusion(f32[512,1024]{1,0:T(8,128)S(1)} %fusion.140, bf16[1664,512]{1,0:T(8,128)(2,1)S(1)} %get-tuple-element.7, bf16[1024,1664]{1,0:T(8,128)(2,1)} %bitcast.37), kind=kOutput, calls=%fused_computation.12 | convolution fusion | flops 1745354752 | bytes 9306112 | tf_op jit(solution)/shard_map/dot_general | solution.py:15
  305.2 3.6 fusion.50
  314.2 3.9 fusion.40
  318.1 3.9 fusion.35
  322.0 3.9 fusion.30
  325.9 3.9 fusion.25
  329.8 3.9 fusion.20
  333.7 3.9 fusion.15
  340.0 4.2 fusion.10
  344.2 3.5 fusion.5
  355.7 3.7 all-to-all-start.2
  359.4 4.0 add_bitcast_fusion
  365.2 31.1 %all-to-all-done.2 = f32[4,4,384,128]{3,2,1,0:T(8,128)S(1)} async-done(((f32[4,4,384,128]{3,2,1,0:T(8,128)}), f32[4,4,384,128]{3,2,1,0:T(8,128)S(1)}, u32[]{:S(2)}, u32[]{:S(2)}) %all-to-all-start.2) | async-done | bytes 3145760 | tf_op jit(solution)/shard_map/all_to_all | solution.py:29
  396.4 4.6 all-to-all-start.6
  402.1 35.2 %all-to-all-done.6 = f32[4,4,384,128]{3,2,1,0:T(8,128)} async-done(((f32[4,4,384,128]{3,2,1,0:T(8,128)}), f32[4,4,384,128]{3,2,1,0:T(8,128)}, u32[]{:S(2)}, u32[]{:S(2)}) %all-to-all-start.6) | async-done | bytes 3145760 | tf_op jit(solution)/shard_map/all_to_all | solution.py:29
  437.3 3.5 all-to-all-start.3
  443.8 16.6 %all-to-all-done.3 = f32[4,384,128]{2,1,0:T(8,128)S(1)} async-done(((f32[4,384,128]{2,1,0:T(8,128)}), f32[4,384,128]{2,1,0:T(8,128)S(1)}, u32[]{:S(2)}, u32[]{:S(2)}) %all-to-all-start.3) | async-done | bytes 786464 | tf_op jit(solution)/shard_map/all_to_all | solution.py:39
  460.4 3.5 all-to-all-start.7
  464.0 19.6 %all-to-all-done.7 = f32[4,384,128]{2,1,0:T(8,128)S(1)} async-done(((f32[4,384,128]{2,1,0:T(8,128)}), f32[4,384,128]{2,1,0:T(8,128)S(1)}, u32[]{:S(2)}, u32[]{:S(2)}) %all-to-all-start.7) | async-done | bytes 786464 | tf_op jit(solution)/shard_map/all_to_all | solution.py:39
  488.0 5.0 all-to-all-done.4
  493.7 3.6 all-to-all-start.8
  497.4 5.3 %all-to-all-done.8 = f32[4,128,128]{2,1,0:T(8,128)S(1)} async-done(((f32[4,128,128]{2,1,0:T(8,128)}), f32[4,128,128]{2,1,0:T(8,128)S(1)}, u32[]{:S(2)}, u32[]{:S(2)}) %all-to-all-start.8) | async-done | bytes 262176 | tf_op jit(solution)/shard_map/all_to_all | solution.py:92
  503.5 4.2 copy.40
  (196 shorter events, 120.2 us)
Async XLA Ops:
  6.5 496.2 %copy-start = (f32[256,256]{1,0:T(8,128)S(1)}, f32[256,256]{1,0:T(8,128)}, u32[]{:S(2)}) copy-start(f32[256,256]{1,0:T(8,128)} %param.13) | copy-start | bytes 786436
  97.5 4.6 copy-start.22
  97.5 81.7 %all-to-all-start.5 = ((bf16[8,1664,128]{2,1,0:T(8,128)(2,1)}), bf16[8,1664,128]{2,1,0:T(8,128)(2,1)}, u32[]{:S(2)}, u32[]{:S(2)}) async-start(bf16[8,1664,128]{2,1,0:T(8,128)(2,1)} %bitcast.279), calls=%async_computation.6 | async-start | bytes 6815744 | tf_op jit(solution)/shard_map/all_to_all | solution.py:75
  113.5 6.0 %copy-start.1 = (bf16[1664,512]{1,0:T(8,128)(2,1)}, bf16[1664,512]{1,0:T(8,128)(2,1)S(1)}, u32[]{:S(2)}) copy-start(bf16[1664,512]{1,0:T(8,128)(2,1)S(1)} %get-tuple-element.8) | copy-start | bytes 5111812
  179.2 81.7 %all-to-all-start = ((bf16[32,32,1664]{2,0,1:T(8,128)(2,1)}), bf16[32,32,1664]{2,0,1:T(8,128)(2,1)}, u32[]{:S(2)}, u32[]{:S(2)}) async-start(bf16[32,32,1664]{2,0,1:T(8,128)(2,1)} %bitcast.278), calls=%async_computation | async-start | bytes 6815744 | tf_op jit(solution)/shard_map/all_to_all | solution.py:47
  182.8 154.7 %reduce-scatter.2.cloned.1.call-start = ((), (), s32[]{:S(2)}) async-start(), calls=%async_computation.10 | async-start | bytes 3932160 | tf_op jit(solution)/shard_map/reduce_scatter | solution.py:62
  195.4 3.5 copy-start.4
  195.4 3.5 copy-start.28
  271.0 3.2 copy-start.43
  278.6 224.9 %all-gather.3.cloned.1.call-start = ((), (), s32[]{:S(2)}) async-start(), calls=%async_computation.11 | async-start | bytes 7077888 | tf_op jit(solution)/shard_map/all_gather | solution.py:62
  281.2 4.9 copy-start.5
  305.2 6.9 %copy-start.6 = (f32[1,4,384,128]{3,2,1,0:T(8,128)}, f32[1,4,384,128]{3,2,1,0:T(8,128)S(1)}, u32[]{:S(2)}) copy-start(f32[1,4,384,128]{3,2,1,0:T(8,128)S(1)} %get-tuple-element.27) | copy-start | bytes 2359300
  305.2 6.9 %copy-start.8 = (f32[1,4,384,128]{3,2,1,0:T(8,128)}, f32[1,4,384,128]{3,2,1,0:T(8,128)S(1)}, u32[]{:S(2)}) copy-start(f32[1,4,384,128]{3,2,1,0:T(8,128)S(1)} %get-tuple-element.28) | copy-start | bytes 2359300
  314.2 36.5 %collective-permute-start = (f32[4,4,384,128]{3,2,1,0:T(8,128)}, f32[4,4,384,128]{3,2,1,0:T(8,128)}, u32[]{:S(2)}, u32[]{:S(2)}) collective-permute-start(f32[4,4,384,128]{3,2,1,0:T(8,128)} %fusion.2), channel_id=1, source_target_pairs={{0,1},{1,0},{2,3},{3,2},{4,5},{5,4},{6,7},{7,6},{8,9},{9,8},{10,11... | collective-permute-start | bytes 9437192 | tf_op jit(solution)/shard_map/ppermute | solution.py:36
  339.3 8.6 %copy-start.14 = (f32[1,4,384,128]{3,2,1,0:T(8,128)}, f32[1,4,384,128]{3,2,1,0:T(8,128)S(1)}, u32[]{:S(2)}) copy-start(f32[1,4,384,128]{3,2,1,0:T(8,128)S(1)} %get-tuple-element.15) | copy-start | bytes 2359300
  339.3 8.6 %copy-start.15 = (f32[1,4,384,128]{3,2,1,0:T(8,128)}, f32[1,4,384,128]{3,2,1,0:T(8,128)S(1)}, u32[]{:S(2)}) copy-start(f32[1,4,384,128]{3,2,1,0:T(8,128)S(1)} %get-tuple-element.16) | copy-start | bytes 2359300
  339.5 8.4 %copy-start.16 = (f32[1,4,384,128]{3,2,1,0:T(8,128)}, f32[1,4,384,128]{3,2,1,0:T(8,128)S(1)}, u32[]{:S(2)}) copy-start(f32[1,4,384,128]{3,2,1,0:T(8,128)S(1)} %get-tuple-element.17) | copy-start | bytes 2359300
  339.5 8.4 %copy-start.17 = (f32[1,4,384,128]{3,2,1,0:T(8,128)}, f32[1,4,384,128]{3,2,1,0:T(8,128)S(1)}, u32[]{:S(2)}) copy-start(f32[1,4,384,128]{3,2,1,0:T(8,128)S(1)} %get-tuple-element.18) | copy-start | bytes 2359300
  340.0 8.0 %copy-start.18 = (f32[1,4,384,128]{3,2,1,0:T(8,128)}, f32[1,4,384,128]{3,2,1,0:T(8,128)S(1)}, u32[]{:S(2)}) copy-start(f32[1,4,384,128]{3,2,1,0:T(8,128)S(1)} %get-tuple-element.19) | copy-start | bytes 2359300
  340.0 8.0 %copy-start.19 = (f32[1,4,384,128]{3,2,1,0:T(8,128)}, f32[1,4,384,128]{3,2,1,0:T(8,128)S(1)}, u32[]{:S(2)}) copy-start(f32[1,4,384,128]{3,2,1,0:T(8,128)S(1)} %get-tuple-element.20) | copy-start | bytes 2359300
  344.2 3.5 copy-start.33
  344.2 3.5 copy-start.34
  348.0 3.2 copy-start.11
  348.0 3.5 copy-start.13
  350.3 9.1 %collective-permute-start.1 = (f32[4,4,384,128]{3,2,1,0:T(8,128)}, f32[4,4,384,128]{3,2,1,0:T(8,128)}, u32[]{:S(2)}, u32[]{:S(2)}) collective-permute-start(f32[4,4,384,128]{3,2,1,0:T(8,128)} %fusion.1), channel_id=1, source_target_pairs={{0,1},{1,0},{2,3},{3,2},{4,5},{5,4},{6,7},{7,6},{8,9},{9,8},{10,11... | collective-permute-start | bytes 9437192 | tf_op jit(solution)/shard_map/ppermute | solution.py:36
  355.7 40.7 %all-to-all-start.2 = ((f32[4,4,384,128]{3,2,1,0:T(8,128)}), f32[4,4,384,128]{3,2,1,0:T(8,128)S(1)}, u32[]{:S(2)}, u32[]{:S(2)}) async-start(f32[4,4,384,128]{3,2,1,0:T(8,128)} %copy.29), calls=%async_computation.2 | async-start | bytes 6291456 | tf_op jit(solution)/shard_map/all_to_all | solution.py:29
  396.4 41.0 %all-to-all-start.6 = ((f32[4,4,384,128]{3,2,1,0:T(8,128)}), f32[4,4,384,128]{3,2,1,0:T(8,128)}, u32[]{:S(2)}, u32[]{:S(2)}) async-start(f32[4,4,384,128]{3,2,1,0:T(8,128)} %copy.33), calls=%async_computation.7 | async-start | bytes 6291456 | tf_op jit(solution)/shard_map/all_to_all | solution.py:29
  437.3 23.1 %all-to-all-start.3 = ((f32[4,384,128]{2,1,0:T(8,128)}), f32[4,384,128]{2,1,0:T(8,128)S(1)}, u32[]{:S(2)}, u32[]{:S(2)}) async-start(f32[4,384,128]{2,1,0:T(8,128)} %reduce_sum.45), calls=%async_computation.3 | async-start | bytes 1572864 | tf_op jit(solution)/shard_map/all_to_all | solution.py:39
  440.8 46.9 %copy-start.45 = (f32[256]{0:T(256)S(1)}, f32[256]{0:T(256)}, u32[]{:S(2)}) copy-start(f32[256]{0:T(256)} %param.9) | copy-start | bytes 3076
  460.4 23.1 %all-to-all-start.7 = ((f32[4,384,128]{2,1,0:T(8,128)}), f32[4,384,128]{2,1,0:T(8,128)S(1)}, u32[]{:S(2)}, u32[]{:S(2)}) async-start(f32[4,384,128]{2,1,0:T(8,128)} %reduce_sum.48), calls=%async_computation.8 | async-start | bytes 1572864 | tf_op jit(solution)/shard_map/all_to_all | solution.py:39
  484.2 8.8 %all-to-all-start.4 = ((f32[4,128,128]{2,1,0:T(8,128)}), f32[4,128,128]{2,1,0:T(8,128)S(1)}, u32[]{:S(2)}, u32[]{:S(2)}) async-start(f32[4,128,128]{2,1,0:T(8,128)} %broadcast_in_dim.10), calls=%async_computation.5 | async-start | bytes 524288 | tf_op jit(solution)/shard_map/all_to_all | solution.py:92
  493.7 8.9 %all-to-all-start.8 = ((f32[4,128,128]{2,1,0:T(8,128)}), f32[4,128,128]{2,1,0:T(8,128)S(1)}, u32[]{:S(2)}, u32[]{:S(2)}) async-start(f32[4,128,128]{2,1,0:T(8,128)} %broadcast_in_dim.11), calls=%async_computation.9 | async-start | bytes 524288 | tf_op jit(solution)/shard_map/all_to_all | solution.py:92
  (26 other events, 62.7 us)
Sparse Core Ops, SparseCore 0:
  278.7 41.5 reduce-scatter.1
  337.7 62.8 all-gather.2
